TPU v7x, 32 devices: a whole 2x2x4 slice. The times are simulated.
32 devices in a mesh: row: 8 (over z, core), col: 4 (over y, x).
Axes of the slice: x: 2, y: 2, z: 4, core: 2. Of those that a mesh axis runs over, the one named last changes fastest.
Arguments:
- matrix_tiles: float32 [10, 8, 128, 20, 4, 128], P(None, 'row', None, None, 'col'), may hold values from -60715.73 to 60715.73
Outputs:
- reduced: float32 [10, 8, 128, 20, 4, 128], P(None, 'row', None, None, 'col')
All inputs are finite; a program needn't handle non-finite values.
Results may differ from a plain program's by a relative error of at most 0.0003.
Values sent between devices are 32-bit elements; how exact they have to be, the bound alone decides.
A program may use at most 128 MiB of HBM per device.

v0:
```python
import jax
import jax.numpy as jnp
from jax import lax
from jax.sharding import PartitionSpec as P

BAND = 256
PANELS = 2


def from_root(shard, axis, root):
    mine = lax.axis_index(axis) == root
    return lax.psum(jnp.where(mine, shard, jnp.zeros_like(shard)), axis)


def multiply(first_matrix, second_matrix):
    return jnp.dot(
        first_matrix,
        second_matrix,
        precision=lax.Precision.HIGHEST,
        preferred_element_type=first_matrix.dtype,
    )


def transposed_left(first_matrix, second_matrix):
    return lax.dot_general(
        first_matrix,
        second_matrix,
        (((0,), (0,)), ((), ())),
        precision=lax.Precision.HIGHEST,
        preferred_element_type=first_matrix.dtype,
    )


def transposed_right(first_matrix, second_matrix):
    return lax.dot_general(
        first_matrix,
        second_matrix,
        (((1,), (1,)), ((), ())),
        precision=lax.Precision.HIGHEST,
        preferred_element_type=first_matrix.dtype,
    )


def lower_inverse(matrix):
    factor = jnp.linalg.cholesky(matrix)
    identity = jnp.eye(matrix.shape[0], dtype=matrix.dtype)
    return lax.linalg.triangular_solve(factor, identity, left_side=True, lower=True)


def reflector_factors(gram_matrix, top_panel):
    inverse = lower_inverse(gram_matrix)
    top_basis = transposed_right(top_panel, inverse)
    sign_values = jnp.where(jnp.diagonal(top_basis) >= 0, -1.0, 1.0).astype(top_basis.dtype)
    shifted = top_basis - jnp.diag(sign_values)
    outer_inverse = lower_inverse(transposed_left(shifted, shifted))
    kernel = transposed_left(outer_inverse, outer_inverse)
    transform = -sign_values[:, None] * multiply(shifted, kernel)
    return (inverse, sign_values, transform)


def mirror_order(pieces, block_rows, tile_size):
    stacked = jnp.stack(pieces, 0)
    stacked = stacked.reshape(len(pieces), block_rows, tile_size, stacked.shape[-1])
    return stacked.transpose(1, 0, 2, 3).reshape(-1, stacked.shape[-1])


def on_device(matrix_tiles):
    tile_shape = matrix_tiles.shape
    block_rows = tile_shape[0]
    tile_size = tile_shape[2]
    block_cols = tile_shape[3]
    row_count = block_rows * tile_size
    col_count = block_cols * tile_size
    local_block = matrix_tiles.reshape(row_count, col_count)
    row_devices = lax.axis_size("row")
    col_devices = lax.axis_size("col")
    row_ratio = row_devices // col_devices
    row_index = lax.axis_index("row")
    col_index = lax.axis_index("col")
    positions = jnp.arange(row_count, dtype=jnp.int32)
    global_rows = (
        positions // tile_size * row_devices + row_index
    ) * tile_size + positions % tile_size
    band_columns = jnp.arange(BAND, dtype=jnp.int32)
    panel_tiles = BAND // tile_size
    for panel_index in range(PANELS):
        panel_start = panel_index * BAND
        below_start = panel_start + BAND
        pieces = []
        for offset in range(panel_tiles):
            column_tile = panel_start // tile_size + offset
            local_tile = column_tile // col_devices
            source = local_block[:, local_tile * tile_size : (local_tile + 1) * tile_size]
            pieces.append(from_root(source, "col", column_tile % col_devices))
        panel_rows = jnp.concatenate(pieces, 1)
        panel_rows = jnp.where((global_rows >= below_start)[:, None], panel_rows, 0.0)
        partial_gram = transposed_left(panel_rows, panel_rows)
        gram_matrix = lax.psum(partial_gram, "row")
        blocks = []
        for offset in range(panel_tiles):
            row_tile = below_start // tile_size + offset
            local_tile = row_tile // row_devices
            source = panel_rows[local_tile * tile_size : (local_tile + 1) * tile_size]
            blocks.append(from_root(source, "row", row_tile % row_devices))
        top_panel = jnp.concatenate(blocks, 0)
        inverse, sign_values, transform = reflector_factors(gram_matrix, top_panel)
        sign_places = (global_rows[:, None] - below_start == band_columns[None, :]).astype(
            local_block.dtype
        )
        vec_rows = transposed_right(panel_rows, inverse) - sign_places * sign_values[None, :]
        pieces = []
        for part_index in range(row_ratio):
            pieces.append(from_root(vec_rows, "row", col_index + col_devices * part_index))
        vec_cols = mirror_order(pieces, block_rows, tile_size)
        summed_rows = lax.psum(multiply(local_block, vec_cols), "col")
        applied = multiply(summed_rows, transform)
        inner_term = multiply(transform.T, lax.psum(transposed_left(vec_rows, applied), "row"))
        update_rows = applied - 0.5 * multiply(vec_rows, inner_term)
        column_part = transposed_left(local_block, vec_rows)
        summed_cols = lax.psum(column_part, "row")
        update_cols = multiply(summed_cols, transform) - 0.5 * multiply(vec_cols, inner_term)
        left_factor = jnp.concatenate([vec_rows, update_rows], 1)
        right_factor = jnp.concatenate([update_cols, vec_cols], 1)
        local_block = local_block - transposed_right(left_factor, right_factor)
    return local_block.reshape(tile_shape)


def solution(mesh):
    return jax.shard_map(
        on_device,
        mesh=mesh,
        in_specs=(P(None, "row", None, None, "col", None),),
        out_specs=P(None, "row", None, None, "col", None),
        check_vma=False,
    )
```

profile of v0, /device:TPU:0, one launch (start us, length us, event | category | flops | bytes accessed | tf_op | source)
XLA Modules:
  0.0 1142.7 jit_solution(3032368912725932266)
XLA Ops:
  6.5 102.2 %reduce.8 = f32[10,128,20,128]{3,2,1,0:T(8,128)} reduce(f32[10,1,128,20,1,128]{5,4,3,2,1,0:T(1,128)} %param.4, f32[]{:T(128)} %constant.208), dimensions={1,4}, to_apply=%param.4.reduce_sub_computation | reduce | bytes 26214404 | tf_op args[0]
  108.8 13.6 %copy.28 = f32[160,8,20,128]{3,1,2,0:T(8,128)} copy(f32[160,8,20,128]{3,2,1,0:T(8,128)} %bitcast.198) | data formatting | bytes 26214400
  124.7 59.2 %all-reduce.38.cloned.1.call-done = (f32[1280,128]{1,0:T(8,128)}, f32[1280,128]{1,0:T(8,128)}) async-done(((f32[1280,128]{1,0:T(8,128)}, f32[1280,128]{1,0:T(8,128)}), (f32[1280,128]{1,0:T(8,128)}, f32[1280,128]{1,0:T(8,128)})) %all-reduce.38.cloned.1.call-update) | async-done | bytes 1310736 | tf_op jit(solution)/shard_map/psum | solution.py:12
  189.5 56.5 %all-reduce.34.cloned.1.call-done = (f32[128,256]{1,0:T(8,128)}, f32[128,256]{1,0:T(8,128)}, f32[256,256]{0,1:T(8,128)}) async-done(((f32[128,256]{1,0:T(8,128)}, f32[128,256]{1,0:T(8,128)}, f32[256,256]{0,1:T(8,128)}), (f32[128,256]{1,0:T(8,128)}, f32[128,256]{1,0:T(8,128)}, f32[256,256]{0,1:T(8,128)})) %all-reduce.34.cloned.1.call-update) | async-done | bytes 524304 | tf_op jit(solution)/shard_map/psum | solution.py:12
  248.1 11.7 %cholesky.214 = f32[128,128]{1,0:T(8,128)S(1)} custom-call(f32[128,128]{1,0:T(8,128)S(1)} %cholesky.346), custom_call_target="Cholesky" | custom-call | tf_op jit(solution)/shard_map/jit(cholesky)/cholesky | solution.py:45
  270.2 11.7 %cholesky.231 = f32[128,128]{1,0:T(8,128)S(1)} custom-call(f32[128,128]{1,0:T(8,128)S(1)} %convolution_subtract_fusion.11), custom_call_target="Cholesky" | custom-call | tf_op jit(solution)/shard_map/jit(cholesky)/cholesky | solution.py:45
  288.1 19.7 %custom-call.22 = f32[2,128,128]{1,2,0:T(8,128)S(1)} custom-call(f32[2,128,128]{2,1,0:T(8,128)S(1)} %get-tuple-element.33), custom_call_target="InvertDiagBlocksLowerTriangular" | custom-call | tf_op jit(solution)/shard_map/triangular_solve/custom-call.0 | solution.py:47
  309.1 11.1 gather_fusion
  321.1 11.7 %cholesky.248 = f32[128,128]{1,0:T(8,128)S(1)} custom-call(f32[128,128]{1,0:T(8,128)S(1)} %cholesky.349), custom_call_target="Cholesky" | custom-call | tf_op jit(solution)/shard_map/jit(cholesky)/cholesky | solution.py:45
  343.2 11.7 %cholesky.265 = f32[128,128]{1,0:T(8,128)S(1)} custom-call(f32[128,128]{1,0:T(8,128)S(1)} %convolution_subtract_fusion.10), custom_call_target="Cholesky" | custom-call | tf_op jit(solution)/shard_map/jit(cholesky)/cholesky | solution.py:45
  365.4 19.7 %custom-call.24 = f32[2,128,128]{1,2,0:T(8,128)S(1)} custom-call(f32[2,128,128]{2,1,0:T(8,128)S(1)} %get-tuple-element.34), custom_call_target="InvertDiagBlocksLowerTriangular" | custom-call | tf_op jit(solution)/shard_map/triangular_solve/custom-call.0 | solution.py:47
  385.7 44.1 %all-reduce.32.cloned.1.call-done = (f32[1,10,128,256]{3,2,0,1:T(8,128)}, f32[1,10,128,256]{3,2,0,1:T(8,128)}) async-done(((f32[1,10,128,256]{3,2,0,1:T(8,128)}, f32[1,10,128,256]{3,2,0,1:T(8,128)}), (f32[1,10,128,256]{3,2,0,1:T(8,128)}, f32[1,10,128,256]{3,2,0,1:T(8,128)})) %all-reduce.32.cloned.1.call-update) | async-done | bytes 2621456 | tf_op jit(solution)/shard_map/psum | solution.py:12
  431.7 25.7 %convolution_bitcast_fusion.1 = f32[1280,256]{0,1:T(8,128)} fusion(f32[2560,256]{1,0:T(8,128)S(1)} %bitcast.202, f32[1280,2560]{1,0:T(8,128)} %bitcast.193), kind=kOutput, calls=%fused_computation.30 | convolution fusion | flops 10066329600 | bytes 17039360 | tf_op jit(solution)/shard_map/dot_general | solution.py:16
  458.9 15.8 %convolution_bitcast_fusion = f32[2560,256]{0,1:T(8,128)} fusion(f32[1280,256]{1,0:T(8,128)S(1)} %copy-done.4, f32[1280,2560]{1,0:T(8,128)} %bitcast.194), kind=kOutput, calls=%fused_computation.23 | convolution fusion | flops 10066329600 | bytes 17039360 | tf_op jit(solution)/shard_map/dot_general | solution.py:25
  474.8 38.4 %all-reduce.20.cloned.1.call-done = f32[1280,256]{0,1:T(8,128)} async-done(((f32[1280,256]{0,1:T(8,128)}), f32[1280,256]{0,1:T(8,128)}) %all-reduce.20.cloned.1.call-update) | async-done | bytes 1310736 | tf_op jit(solution)/shard_map/psum | solution.py:115
  523.2 69.6 %all-reduce.30.cloned.1.call-done = (f32[2560,256]{0,1:T(8,128)}, f32[256,256]{1,0:T(8,128)}) async-done(((f32[2560,256]{0,1:T(8,128)}, f32[256,256]{1,0:T(8,128)}), (f32[2560,256]{0,1:T(8,128)}, f32[256,256]{1,0:T(8,128)})) %all-reduce.30.cloned.1.call-update) | async-done | bytes 2883600 | tf_op jit(solution)/shard_map/psum | solution.py:120
  604.0 24.8 %convolution_subtract_fusion.1 = f32[1280,2560]{1,0:T(8,128)S(1)} fusion(f32[1280,2560]{1,0:T(8,128)} %bitcast.195, f32[2560,256]{1,0:T(8,128)S(1)} %bitcast.204, f32[2560,256]{1,0:T(8,128)S(1)} %fusion.7, f32[1280,256]{1,0:T(8,128)S(1)} %fusion.9, f32[1280,256]{1,0:T(8,128)S(1)} %copy-done.6), kind=kOutput, calls=%fused_computation.11 | convolution fusion | flops 20137902080 | bytes 34078720 | tf_op jit(solution)/shard_map/dot_general | solution.py:35
  635.0 56.0 %all-reduce.36.cloned.1.call-done = (f32[1280,128]{1,0:T(8,128)}, f32[1280,128]{1,0:T(8,128)}) async-done(((f32[1280,128]{1,0:T(8,128)}, f32[1280,128]{1,0:T(8,128)}), (f32[1280,128]{1,0:T(8,128)}, f32[1280,128]{1,0:T(8,128)})) %all-reduce.36.cloned.1.call-update) | async-done | bytes 1310736 | tf_op jit(solution)/shard_map/psum | solution.py:12
  696.5 56.6 %all-reduce.28.cloned.1.call-done = (f32[128,256]{1,0:T(8,128)}, f32[128,256]{1,0:T(8,128)}, f32[256,256]{0,1:T(8,128)}) async-done(((f32[128,256]{1,0:T(8,128)}, f32[128,256]{1,0:T(8,128)}, f32[256,256]{0,1:T(8,128)}), (f32[128,256]{1,0:T(8,128)}, f32[128,256]{1,0:T(8,128)}, f32[256,256]{0,1:T(8,128)})) %all-reduce.28.cloned.1.call-update) | async-done | bytes 524304 | tf_op jit(solution)/shard_map/psum | solution.py:12
  755.2 11.7 %cholesky.282 = f32[128,128]{1,0:T(8,128)S(1)} custom-call(f32[128,128]{1,0:T(8,128)S(1)} %cholesky.352), custom_call_target="Cholesky" | custom-call | tf_op jit(solution)/shard_map/jit(cholesky)/cholesky | solution.py:45
  777.3 11.7 %cholesky.299 = f32[128,128]{1,0:T(8,128)S(1)} custom-call(f32[128,128]{1,0:T(8,128)S(1)} %convolution_subtract_fusion.9), custom_call_target="Cholesky" | custom-call | tf_op jit(solution)/shard_map/jit(cholesky)/cholesky | solution.py:45
  795.8 19.7 %custom-call.26 = f32[2,128,128]{1,2,0:T(8,128)S(1)} custom-call(f32[2,128,128]{2,1,0:T(8,128)S(1)} %get-tuple-element.35), custom_call_target="InvertDiagBlocksLowerTriangular" | custom-call | tf_op jit(solution)/shard_map/triangular_solve/custom-call.0 | solution.py:47
  820.2 11.7 %cholesky.316 = f32[128,128]{1,0:T(8,128)S(1)} custom-call(f32[128,128]{1,0:T(8,128)S(1)} %cholesky.355), custom_call_target="Cholesky" | custom-call | tf_op jit(solution)/shard_map/jit(cholesky)/cholesky | solution.py:45
  842.3 11.7 %cholesky.333 = f32[128,128]{1,0:T(8,128)S(1)} custom-call(f32[128,128]{1,0:T(8,128)S(1)} %convolution_subtract_fusion.8), custom_call_target="Cholesky" | custom-call | tf_op jit(solution)/shard_map/jit(cholesky)/cholesky | solution.py:45
  864.6 19.7 %custom-call.28 = f32[2,128,128]{1,2,0:T(8,128)S(1)} custom-call(f32[2,128,128]{2,1,0:T(8,128)S(1)} %get-tuple-element.36), custom_call_target="InvertDiagBlocksLowerTriangular" | custom-call | tf_op jit(solution)/shard_map/triangular_solve/custom-call.0 | solution.py:47
  884.9 44.1 %all-reduce.26.cloned.1.call-done = (f32[1,10,128,256]{3,2,0,1:T(8,128)}, f32[1,10,128,256]{3,2,0,1:T(8,128)}) async-done(((f32[1,10,128,256]{3,2,0,1:T(8,128)}, f32[1,10,128,256]{3,2,0,1:T(8,128)}), (f32[1,10,128,256]{3,2,0,1:T(8,128)}, f32[1,10,128,256]{3,2,0,1:T(8,128)})) %all-reduce.26.cloned.1.call-update) | async-done | bytes 2621456 | tf_op jit(solution)/shard_map/psum | solution.py:12
  930.9 14.3 %fusion.110 = f32[1280,256]{1,0:T(8,128)} fusion(f32[1280,2560]{1,0:T(8,128)} %copy-done, f32[2560,256]{1,0:T(8,128)S(1)} %bitcast.199), kind=kOutput, calls=%fused_computation.223 | convolution fusion | flops 10066329600 | bytes 17039360 | tf_op jit(solution)/shard_map/dot_general | solution.py:16
  946.6 25.0 %fusion.114 = f32[2560,256]{1,0:T(8,128)} fusion(f32[1280,2560]{1,0:T(8,128)} %copy-done, f32[1280,256]{1,0:T(8,128)S(1)} %copy-done.1), kind=kOutput, calls=%fused_computation.227 | convolution fusion | flops 10066329600 | bytes 17039360 | tf_op jit(solution)/shard_map/dot_general | solution.py:25
  971.7 29.2 %all-reduce.22.cloned.1.call-done = f32[1280,256]{1,0:T(8,128)} async-done(((f32[1280,256]{1,0:T(8,128)}), f32[1280,256]{1,0:T(8,128)}) %all-reduce.22.cloned.1.call-update) | async-done | bytes 1310736 | tf_op jit(solution)/shard_map/psum | solution.py:115
  1010.6 69.9 %all-reduce.24.cloned.1.call-done = (f32[2560,256]{1,0:T(8,128)}, f32[256,256]{1,0:T(8,128)}) async-done(((f32[2560,256]{1,0:T(8,128)}, f32[256,256]{1,0:T(8,128)}), (f32[2560,256]{1,0:T(8,128)}, f32[256,256]{1,0:T(8,128)})) %all-reduce.24.cloned.1.call-update) | async-done | bytes 2883600 | tf_op jit(solution)/shard_map/psum | solution.py:120
  1089.8 25.8 %convolution_subtract_fusion = f32[1280,2560]{1,0:T(8,128)} fusion(f32[1280,2560]{1,0:T(8,128)} %copy-done, f32[2560,256]{1,0:T(8,128)S(1)} %bitcast.201, f32[2560,256]{1,0:T(8,128)S(1)} %fusion.6, f32[1280,256]{1,0:T(8,128)S(1)} %fusion.8, f32[1280,256]{1,0:T(8,128)S(1)} %copy-done.3), kind=kOutput, calls=%fused_computation.10 | convolution fusion | flops 20137902080 | bytes 34078720 | tf_op jit(solution)/shard_map/dot_general | solution.py:35
  1115.6 19.9 %reshape.157 = f32[10,1,128,20,1,128]{5,4,3,2,1,0:T(1,128)} reshape(f32[1280,2560]{1,0:T(8,128)} %convolution_subtract_fusion) | data formatting | bytes 26214400 | tf_op jit(solution)/shard_map/reshape | solution.py:125
  (186 shorter events, 164.8 us)
Async XLA Ops:
  6.5 177.3 %all-reduce.38.cloned.1.call-start = ((), (), s32[]{:S(2)}) async-start(), calls=%async_computation.9 | async-start | bytes 2621440 | tf_op jit(solution)/shard_map/psum | solution.py:12
  124.6 121.4 %all-reduce.34.cloned.1.call-start = ((), (), s32[]{:S(2)}) async-start(), calls=%async_computation.7 | async-start | bytes 1048576 | tf_op jit(solution)/shard_map/psum | solution.py:12
  189.1 240.6 %all-reduce.32.cloned.1.call-start = ((), (), s32[]{:S(2)}) async-start(), calls=%async_computation.6 | async-start | bytes 5242880 | tf_op jit(solution)/shard_map/psum | solution.py:12
  281.9 26.7 %copy-start.11 = (f32[128,256]{1,0:T(8,128)S(1)}, f32[128,256]{1,0:T(8,128)}, u32[]{:S(2)}) copy-start(f32[128,256]{1,0:T(8,128)} %get-tuple-element.80) | copy-start | bytes 393220
  281.9 26.7 %copy-start.12 = (f32[128,256]{1,0:T(8,128)S(1)}, f32[128,256]{1,0:T(8,128)}, u32[]{:S(2)}) copy-start(f32[128,256]{1,0:T(8,128)} %get-tuple-element.81) | copy-start | bytes 393220
  361.2 152.0 %all-reduce.20.cloned.1.call-start = ((), (), s32[]{:S(2)}) async-start(), calls=%async_computation | async-start | bytes 2621440 | tf_op jit(solution)/shard_map/psum | solution.py:115
  457.5 135.3 %all-reduce.30.cloned.1.call-start = ((), (), s32[]{:S(2)}) async-start(), calls=%async_computation.5 | async-start | bytes 5767168 | tf_op jit(solution)/shard_map/psum | solution.py:120
  457.6 1.4 copy-start.4
  513.2 3.9 copy-start.5
  516.0 1.1 copy-start.7
  520.1 170.8 %all-reduce.36.cloned.1.call-start = ((), (), s32[]{:S(2)}) async-start(), calls=%async_computation.8 | async-start | bytes 2621440 | tf_op jit(solution)/shard_map/psum | solution.py:12
  594.3 6.2 copy-start.6
  594.4 6.2 copy-start.9
  628.8 5.0 copy-start
  634.9 118.2 %all-reduce.28.cloned.1.call-start = ((), (), s32[]{:S(2)}) async-start(), calls=%async_computation.4 | async-start | bytes 1048576 | tf_op jit(solution)/shard_map/psum | solution.py:12
  696.2 232.7 %all-reduce.26.cloned.1.call-start = ((), (), s32[]{:S(2)}) async-start(), calls=%async_computation.3 | async-start | bytes 5242880 | tf_op jit(solution)/shard_map/psum | solution.py:12
  789.0 27.3 %copy-start.13 = (f32[128,256]{1,0:T(8,128)S(1)}, f32[128,256]{1,0:T(8,128)}, u32[]{:S(2)}) copy-start(f32[128,256]{1,0:T(8,128)} %get-tuple-element.73) | copy-start | bytes 393220
  789.0 27.3 %copy-start.14 = (f32[128,256]{1,0:T(8,128)S(1)}, f32[128,256]{1,0:T(8,128)}, u32[]{:S(2)}) copy-start(f32[128,256]{1,0:T(8,128)} %get-tuple-element.74) | copy-start | bytes 393220
  860.3 140.5 %all-reduce.22.cloned.1.call-start = ((), (), s32[]{:S(2)}) async-start(), calls=%async_computation.1 | async-start | bytes 2621440 | tf_op jit(solution)/shard_map/psum | solution.py:115
  945.2 135.3 %all-reduce.24.cloned.1.call-start = ((), (), s32[]{:S(2)}) async-start(), calls=%async_computation.2 | async-start | bytes 5767168 | tf_op jit(solution)/shard_map/psum | solution.py:120
  945.3 1.4 copy-start.1
  1000.9 3.9 copy-start.2
  1003.7 1.1 copy-start.8
  1082.0 4.2 copy-start.3
  1082.0 4.2 copy-start.10
Sparse Core Ops, SparseCore 0:
  124.7 59.0 all-reduce.37
  189.3 56.7 all-reduce.33
  361.3 68.3 all-reduce.31
  457.6 55.5 all-reduce.19
  520.3 72.4 all-reduce.29
  635.0 55.8 all-reduce.35
  696.3 56.7 all-reduce.27
  860.5 68.4 all-reduce.25
  945.3 55.5 all-reduce.21
  1008.0 72.4 all-reduce.23
where the time goes:
time: 1150 us; the launch traced here: 1140 us
  waiting for transfers between devices  524 us (46%)
  other arithmetic  333 us (29%)
  matrix products  186 us (16%)
  local copies, waits for them, and re-layouts  78.6 us (7%)
  between operations  19.9 us (2%)
    psum x6, waiting for transfers between devices, from_root(): return lax.psum(jnp.where(mine, shard, jnp.zeros_like(shard)), axis)  316 us
    psum x2, waiting for transfers between devices, on_device(): summed_cols = lax.psum(column_part, 'row')  139 us
    another operation x27, other arithmetic, lower_inverse(): factor = jnp.linalg.cholesky(matrix)  138 us
    unnamed x1, other arithmetic  102 us
    another operation x9, other arithmetic, lower_inverse(): lax.linalg.triangular_solve(factor, identity, left_side=True, lower=True)  78.8 us
    psum x2, waiting for transfers between devices, on_device(): summed_rows = lax.psum(multiply(local_block, vec_cols), 'col')  67.6 us
    dot_general x14, matrix products, multiply(): jnp.dot(first_matrix, second_matrix, precision=lax.Precision.HIGHEST, pre...  66.7 us
    dot_general x6, matrix products, transposed_right(): lax.dot_general(first_matrix, second_matrix, (((1,), (1,)), ((), ())), pr...  58.7 us
  transfers between devices with their start and end apart: 10, of which 10 were waited for; matrix products, arithmetic and copies ran while one was open for 9% of the time, Pallas kernels for 0%

commit v1 on v0

--- a/solution.py
+++ b/solution.py
@@ -117,7 +117,8 @@
         inner_term = multiply(transform.T, lax.psum(transposed_left(vec_rows, applied), "row"))
         update_rows = applied - 0.5 * multiply(vec_rows, inner_term)
         column_part = transposed_left(local_block, vec_rows)
-        summed_cols = lax.psum(column_part, "row")
+        a_next = jax.lax.all_gather(column_part, "row")
+        summed_cols = jnp.sum(a_next, 0)
         update_cols = multiply(summed_cols, transform) - 0.5 * multiply(vec_cols, inner_term)
         left_factor = jnp.concatenate([vec_rows, update_rows], 1)
         right_factor = jnp.concatenate([update_cols, vec_cols], 1)

time: 1150 us -> 1440 us (1.25)
  waiting for transfers between devices: 524 us -> 767 us
  local copies, waits for them, and re-layouts: 78.6 us -> 100 us
  other arithmetic: 333 us -> 353 us
    all_gather x0 -> x2, waiting for transfers between devices: none -> 362 us  [on_device(): a_next = jax.lax.all_gather(column_part, 'row')]
    psum x2, waiting for transfers between devices: 139 us -> 60.6 us  [on_device(): lax.psum(transposed_left(vec_rows, applied), 'row')]
    psum x6, waiting for transfers between devices: 316 us -> 290 us  [from_root(): return lax.psum(jnp.where(mine, shard, jnp.zeros_like(shard)), axis)]
    unnamed x31 -> x52, local copies, waits for them, and re-layouts: 20.8 us -> 44.8 us
    reduce_sum x0 -> x2, other arithmetic: none -> 18.6 us  [on_device(): summed_cols = jnp.sum(a_next, 0)]
    unnamed x1 -> x2, other arithmetic: 102 us -> 102 us
  transfers between devices with their start and end apart: 10 -> 12, of which waited for: 10 -> 12; matrix products, arithmetic and copies ran while one was open for 9% -> 13% of each run, Pallas kernels for 0% -> 0%
where the time goes in v1:
time: 1440 us; the launch traced here: 1430 us
  waiting for transfers between devices  767 us (53%)
  other arithmetic  353 us (25%)
  matrix products  189 us (13%)
  local copies, waits for them, and re-layouts  100 us (7%)
  between operations  19.7 us (1%)
    all_gather x2, waiting for transfers between devices, on_device(): a_next = jax.lax.all_gather(column_part, 'row')  362 us
    psum x6, waiting for transfers between devices, from_root(): return lax.psum(jnp.where(mine, shard, jnp.zeros_like(shard)), axis)  290 us
    another operation x27, other arithmetic, lower_inverse(): factor = jnp.linalg.cholesky(matrix)  138 us
    unnamed x2, other arithmetic  102 us
    another operation x9, other arithmetic, lower_inverse(): lax.linalg.triangular_solve(factor, identity, left_side=True, lower=True)  80.2 us
    dot_general x14, matrix products, multiply(): jnp.dot(first_matrix, second_matrix, precision=lax.Precision.HIGHEST, pre...  72.1 us
    psum x2, waiting for transfers between devices, on_device(): lax.psum(transposed_left(vec_rows, applied), 'row')  60.6 us
    dot_general x10, matrix products, transposed_left(): lax.dot_general(first_matrix, second_matrix, (((0,), (0,)), ((), ())), pr...  55.4 us
  transfers between devices with their start and end apart: 12, of which 12 were waited for; matrix products, arithmetic and copies ran while one was open for 13% of the time, Pallas kernels for 0%

profile of v1, /device:TPU:0, one launch (start us, length us, event | category | flops | bytes accessed | tf_op | source)
XLA Modules:
  0.0 1430.5 jit_solution(17366650871920736703)
XLA Ops:
  6.5 102.2 %reduce.8 = f32[10,128,20,128]{3,2,1,0:T(8,128)} reduce(f32[10,1,128,20,1,128]{5,4,3,2,1,0:T(1,128)} %param.4, f32[]{:T(128)} %constant.208), dimensions={1,4}, to_apply=%param.4.reduce_sub_computation | reduce | bytes 26214404 | tf_op args[0]
  108.8 13.6 copy.48
  124.7 59.2 %all-reduce.36.cloned.1.call-done = (f32[1280,128]{1,0:T(8,128)}, f32[1280,128]{1,0:T(8,128)}) async-done(((f32[1280,128]{1,0:T(8,128)}, f32[1280,128]{1,0:T(8,128)}), (f32[1280,128]{1,0:T(8,128)}, f32[1280,128]{1,0:T(8,128)})) %all-reduce.36.cloned.1.call-update) | async-done | bytes 1310736 | tf_op jit(solution)/shard_map/psum | solution.py:12
  189.7 56.3 %all-reduce.32.cloned.1.call-done = (f32[128,256]{1,0:T(8,128)}, f32[128,256]{1,0:T(8,128)}, f32[256,256]{0,1:T(8,128)}) async-done(((f32[128,256]{1,0:T(8,128)}, f32[128,256]{1,0:T(8,128)}, f32[256,256]{0,1:T(8,128)}), (f32[128,256]{1,0:T(8,128)}, f32[128,256]{1,0:T(8,128)}, f32[256,256]{0,1:T(8,128)})) %all-reduce.32.cloned.1.call-update) | async-done | bytes 524304 | tf_op jit(solution)/shard_map/psum | solution.py:12
  248.1 11.7 cholesky.214
  270.2 11.7 cholesky.231
  288.1 19.7 %custom-call.22 = f32[2,128,128]{1,2,0:T(8,128)S(1)} custom-call(f32[2,128,128]{2,1,0:T(8,128)S(1)} %get-tuple-element.33), custom_call_target="InvertDiagBlocksLowerTriangular" | custom-call | tf_op jit(solution)/shard_map/triangular_solve/custom-call.0 | solution.py:47
  316.0 11.7 cholesky.248
  338.0 11.7 cholesky.265
  352.9 31.4 %all-reduce.30.cloned.1.call-done = (f32[1,10,128,256]{3,2,0,1:T(8,128)}, f32[1,10,128,256]{3,2,0,1:T(8,128)}) async-done(((f32[1,10,128,256]{3,2,0,1:T(8,128)}, f32[1,10,128,256]{3,2,0,1:T(8,128)}), (f32[1,10,128,256]{3,2,0,1:T(8,128)}, f32[1,10,128,256]{3,2,0,1:T(8,128)})) %all-reduce.30.cloned.1.call-update) | async-done | bytes 2621456 | tf_op jit(solution)/shard_map/psum | solution.py:12
  386.3 26.8 %convolution_bitcast_fusion.1 = f32[1280,256]{0,1:T(8,128)} fusion(f32[2560,256]{1,0:T(8,128)S(1)} %bitcast.210, f32[1280,2560]{1,0:T(8,128)} %bitcast.199), kind=kOutput, calls=%fused_computation.31 | convolution fusion | flops 10066329600 | bytes 17039360 | tf_op jit(solution)/shard_map/dot_general | solution.py:16
  419.0 19.7 %custom-call.24 = f32[2,128,128]{1,2,0:T(8,128)S(1)} custom-call(f32[2,128,128]{2,1,0:T(8,128)S(1)} %get-tuple-element.34), custom_call_target="InvertDiagBlocksLowerTriangular" | custom-call | tf_op jit(solution)/shard_map/triangular_solve/custom-call.0 | solution.py:47
  442.2 26.7 %all-reduce.18.cloned.1.call-done = f32[1280,256]{0,1:T(8,128)} async-done(((f32[1280,256]{0,1:T(8,128)}), f32[1280,256]{0,1:T(8,128)}) %all-reduce.18.cloned.1.call-update) | async-done | bytes 1310736 | tf_op jit(solution)/shard_map/psum | solution.py:115
  475.8 15.5 %convolution_bitcast_fusion = f32[2560,256]{0,1:T(8,128)} fusion(f32[1280,256]{1,0:T(8,128)} %get-tuple-element.125, f32[1280,2560]{1,0:T(8,128)} %bitcast.200), kind=kOutput, calls=%fused_computation.24 | convolution fusion | flops 10066329600 | bytes 17039360 | tf_op jit(solution)/shard_map/dot_general | solution.py:25
  495.6 35.8 %all-reduce.20.cloned.1.call-done = f32[256,256]{1,0:T(8,128)} async-done(((f32[256,256]{1,0:T(8,128)}), f32[256,256]{1,0:T(8,128)}) %all-reduce.20.cloned.1.call-update) | async-done | bytes 262160 | tf_op jit(solution)/shard_map/psum | solution.py:117
  536.0 181.4 %all-gather.5.cloned.1.call-done = f32[20480,256]{0,1:T(8,128)} async-done(((f32[2560,256]{0,1:T(8,128)}), f32[20480,256]{0,1:T(8,128)}) %all-gather.5.cloned.1.call-update) | async-done | bytes 20971536 | tf_op jit(solution)/shard_map/all_gather | solution.py:120
  717.4 23.4 %copy.46 = f32[32,8,8,2560]{3,2,1,0:T(8,128)S(1)} copy(f32[32,8,8,2560]{3,1,2,0:T(8,128)} %bitcast.213) | data formatting | bytes 41943040
  757.0 21.5 %convolution_subtract_fusion.1 = f32[1280,2560]{1,0:T(8,128)S(1)} fusion(f32[1280,2560]{1,0:T(8,128)S(1)} %bitcast.203, f32[2560,256]{0,1:T(8,128)S(1)} %copy-done.9, f32[2560,256]{0,1:T(8,128)S(1)} %fusion.7, f32[1280,256]{1,0:T(8,128)S(1)} %copy-done.11, f32[1280,256]{1,0:T(8,128)S(1)} %copy-done.4), kind=kOutput, calls=%fused_computation.12 | convolution fusion | flops 20137902080 | bytes 34078720 | tf_op jit(solution)/shard_map/dot_general | solution.py:35
  784.7 54.6 %all-reduce.34.cloned.1.call-done = (f32[1280,128]{1,0:T(8,128)}, f32[1280,128]{1,0:T(8,128)}) async-done(((f32[1280,128]{1,0:T(8,128)}, f32[1280,128]{1,0:T(8,128)}), (f32[1280,128]{1,0:T(8,128)}, f32[1280,128]{1,0:T(8,128)})) %all-reduce.34.cloned.1.call-update) | async-done | bytes 1310736 | tf_op jit(solution)/shard_map/psum | solution.py:12
  844.6 56.8 %all-reduce.28.cloned.1.call-done = (f32[128,256]{1,0:T(8,128)}, f32[128,256]{1,0:T(8,128)}, f32[256,256]{0,1:T(8,128)}) async-done(((f32[128,256]{1,0:T(8,128)}, f32[128,256]{1,0:T(8,128)}, f32[256,256]{0,1:T(8,128)}), (f32[128,256]{1,0:T(8,128)}, f32[128,256]{1,0:T(8,128)}, f32[256,256]{0,1:T(8,128)})) %all-reduce.28.cloned.1.call-update) | async-done | bytes 524304 | tf_op jit(solution)/shard_map/psum | solution.py:12
  925.6 11.7 cholesky.299
  944.3 19.7 %custom-call.26 = f32[2,128,128]{1,2,0:T(8,128)S(1)} custom-call(f32[2,128,128]{2,1,0:T(8,128)S(1)} %get-tuple-element.35), custom_call_target="InvertDiagBlocksLowerTriangular" | custom-call | tf_op jit(solution)/shard_map/triangular_solve/custom-call.0 | solution.py:47
  994.0 11.7 cholesky.333
  1009.1 31.3 %all-reduce.26.cloned.1.call-done = (f32[1,10,128,256]{3,2,0,1:T(8,128)}, f32[1,10,128,256]{3,2,0,1:T(8,128)}) async-done(((f32[1,10,128,256]{3,2,0,1:T(8,128)}, f32[1,10,128,256]{3,2,0,1:T(8,128)}), (f32[1,10,128,256]{3,2,0,1:T(8,128)}, f32[1,10,128,256]{3,2,0,1:T(8,128)})) %all-reduce.26.cloned.1.call-update) | async-done | bytes 2621456 | tf_op jit(solution)/shard_map/psum | solution.py:12
  1042.3 14.4 %fusion.110 = f32[1280,256]{1,0:T(8,128)} fusion(f32[1280,2560]{1,0:T(8,128)} %copy-done, f32[2560,256]{1,0:T(8,128)S(1)} %bitcast.207), kind=kOutput, calls=%fused_computation.224 | convolution fusion | flops 10066329600 | bytes 17039360 | tf_op jit(solution)/shard_map/dot_general | solution.py:16
  1062.4 19.7 %custom-call.28 = f32[2,128,128]{1,2,0:T(8,128)S(1)} custom-call(f32[2,128,128]{2,1,0:T(8,128)S(1)} %get-tuple-element.36), custom_call_target="InvertDiagBlocksLowerTriangular" | custom-call | tf_op jit(solution)/shard_map/triangular_solve/custom-call.0 | solution.py:47
  1084.9 27.7 %all-reduce.22.cloned.1.call-done = f32[1280,256]{1,0:T(8,128)} async-done(((f32[1280,256]{1,0:T(8,128)}), f32[1280,256]{1,0:T(8,128)}) %all-reduce.22.cloned.1.call-update) | async-done | bytes 1310736 | tf_op jit(solution)/shard_map/psum | solution.py:115
  1119.5 25.3 %fusion.114 = f32[2560,256]{1,0:T(8,128)} fusion(f32[1280,2560]{1,0:T(8,128)} %copy-done, f32[1280,256]{1,0:T(8,128)} %get-tuple-element.130), kind=kOutput, calls=%fused_computation.228 | convolution fusion | flops 10066329600 | bytes 17039360 | tf_op jit(solution)/shard_map/dot_general | solution.py:25
  1150.2 24.8 %all-reduce.24.cloned.1.call-done = f32[256,256]{1,0:T(8,128)} async-done(((f32[256,256]{1,0:T(8,128)}), f32[256,256]{1,0:T(8,128)}) %all-reduce.24.cloned.1.call-update) | async-done | bytes 262160 | tf_op jit(solution)/shard_map/psum | solution.py:117
  1180.6 180.5 %all-gather.7.cloned.1.call-done = f32[20480,256]{1,0:T(8,128)} async-done(((f32[2560,256]{1,0:T(8,128)}), f32[20480,256]{1,0:T(8,128)}) %all-gather.7.cloned.1.call-update) | async-done | bytes 20971536 | tf_op jit(solution)/shard_map/all_gather | solution.py:120
  1377.9 25.7 %convolution_subtract_fusion = f32[1280,2560]{1,0:T(8,128)} fusion(f32[1280,2560]{1,0:T(8,128)} %copy-done, f32[2560,256]{0,1:T(8,128)S(1)} %copy-done.10, f32[2560,256]{0,1:T(8,128)S(1)} %fusion.6, f32[1280,256]{1,0:T(8,128)S(1)} %copy-done.12, f32[1280,256]{1,0:T(8,128)S(1)} %copy-done.6), kind=kOutput, calls=%fused_computation.11 | convolution fusion | flops 20137902080 | bytes 34078720 | tf_op jit(solution)/shard_map/dot_general | solution.py:35
  1403.6 19.9 %reshape.159 = f32[10,1,128,20,1,128]{5,4,3,2,1,0:T(1,128)} reshape(f32[1280,2560]{1,0:T(8,128)} %convolution_subtract_fusion) | data formatting | bytes 26214400 | tf_op jit(solution)/shard_map/reshape | solution.py:126
  (218 shorter events, 226.0 us)
Async XLA Ops:
  6.5 177.4 %all-reduce.36.cloned.1.call-start = ((), (), s32[]{:S(2)}) async-start(), calls=%async_computation.11 | async-start | bytes 2621440 | tf_op jit(solution)/shard_map/psum | solution.py:12
  124.6 121.4 %all-reduce.32.cloned.1.call-start = ((), (), s32[]{:S(2)}) async-start(), calls=%async_computation.9 | async-start | bytes 1048576 | tf_op jit(solution)/shard_map/psum | solution.py:12
  189.2 195.2 %all-reduce.30.cloned.1.call-start = ((), (), s32[]{:S(2)}) async-start(), calls=%async_computation.8 | async-start | bytes 5242880 | tf_op jit(solution)/shard_map/psum | solution.py:12
  281.9 26.8 %copy-start.17 = (f32[128,256]{1,0:T(8,128)S(1)}, f32[128,256]{1,0:T(8,128)}, u32[]{:S(2)}) copy-start(f32[128,256]{1,0:T(8,128)} %get-tuple-element.76) | copy-start | bytes 393220
  281.9 26.8 %copy-start.18 = (f32[128,256]{1,0:T(8,128)S(1)}, f32[128,256]{1,0:T(8,128)}, u32[]{:S(2)}) copy-start(f32[128,256]{1,0:T(8,128)} %get-tuple-element.77) | copy-start | bytes 393220
  315.7 153.2 %all-reduce.18.cloned.1.call-start = ((), (), s32[]{:S(2)}) async-start(), calls=%async_computation | async-start | bytes 2621440 | tf_op jit(solution)/shard_map/psum | solution.py:115
  386.3 105.1 %copy-start.1 = (f32[2,10,128,256]{3,2,0,1:T(8,128)}, f32[2,10,128,256]{3,2,0,1:T(8,128)S(1)}, u32[]{:S(2)}) copy-start(f32[2,10,128,256]{3,2,0,1:T(8,128)S(1)} %pad_maximum_fusion) | copy-start | bytes 7864324
  413.1 118.3 %all-reduce.20.cloned.1.call-start = ((), (), s32[]{:S(2)}) async-start(), calls=%async_computation.1 | async-start | bytes 524288 | tf_op jit(solution)/shard_map/psum | solution.py:117
  468.9 3.8 copy-start.3
  475.8 241.6 %all-gather.5.cloned.1.call-start = ((), (), s32[]{:S(2)}) async-start(), calls=%async_computation.4 | async-start | bytes 23592960 | tf_op jit(solution)/shard_map/all_gather | solution.py:120
  491.4 348.0 %all-reduce.34.cloned.1.call-start = ((), (), s32[]{:S(2)}) async-start(), calls=%async_computation.10 | async-start | bytes 2621440 | tf_op jit(solution)/shard_map/psum | solution.py:12
  493.8 37.6 %copy-start.13 = (f32[256,256]{1,0:T(8,128)S(1)}, f32[256,256]{1,0:T(8,128)}, u32[]{:S(2)}) copy-start(f32[256,256]{1,0:T(8,128)} %convolution_multiply_fusion.5) | copy-start | bytes 786436
  493.8 39.9 %copy-start.4 = (f32[1280,256]{1,0:T(8,128)S(1)}, f32[1280,256]{1,0:T(8,128)}, u32[]{:S(2)}) copy-start(f32[1280,256]{1,0:T(8,128)} %get-tuple-element.125) | copy-start | bytes 3932164
  740.8 8.9 copy-start.14
  740.8 16.1 %slice-start = ((s8[13107200]{0:T(1024)(128)(4,1)}), s8[4194304]{0:T(1024)(128)(4,1)S(1)}, s32[]{:S(2)}) async-start(s8[13107200]{0:T(1024)(128)(4,1)} %bitcast.201), calls=%async_computation.12 | async-start | bytes 8388608
  740.8 16.1 %slice-start.1 = ((s8[13107200]{0:T(1024)(128)(4,1)}), s8[4194304]{0:T(1024)(128)(4,1)S(1)}, s32[]{:S(2)}) async-start(s8[13107200]{0:T(1024)(128)(4,1)} %bitcast.201), calls=%async_computation.13 | async-start | bytes 8388608
  740.8 16.1 %slice-start.2 = ((s8[13107200]{0:T(1024)(128)(4,1)}), s8[4194304]{0:T(1024)(128)(4,1)S(1)}, s32[]{:S(2)}) async-start(s8[13107200]{0:T(1024)(128)(4,1)} %bitcast.201), calls=%async_computation.14 | async-start | bytes 8388608
  749.6 4.5 copy-start.2
  749.6 4.5 copy-start.16
  749.6 7.3 slice-start.3
  754.1 2.8 copy-start.9
  754.2 2.8 copy-start.11
  778.5 5.0 copy-start
  784.6 116.8 %all-reduce.28.cloned.1.call-start = ((), (), s32[]{:S(2)}) async-start(), calls=%async_computation.7 | async-start | bytes 1048576 | tf_op jit(solution)/shard_map/psum | solution.py:12
  844.6 195.8 %all-reduce.26.cloned.1.call-start = ((), (), s32[]{:S(2)}) async-start(), calls=%async_computation.6 | async-start | bytes 5242880 | tf_op jit(solution)/shard_map/psum | solution.py:12
  937.4 27.5 %copy-start.19 = (f32[128,256]{1,0:T(8,128)S(1)}, f32[128,256]{1,0:T(8,128)}, u32[]{:S(2)}) copy-start(f32[128,256]{1,0:T(8,128)} %get-tuple-element.71) | copy-start | bytes 393220
  937.4 27.6 %copy-start.20 = (f32[128,256]{1,0:T(8,128)S(1)}, f32[128,256]{1,0:T(8,128)}, u32[]{:S(2)}) copy-start(f32[128,256]{1,0:T(8,128)} %get-tuple-element.72) | copy-start | bytes 393220
  971.8 140.8 %all-reduce.22.cloned.1.call-start = ((), (), s32[]{:S(2)}) async-start(), calls=%async_computation.2 | async-start | bytes 2621440 | tf_op jit(solution)/shard_map/psum | solution.py:115
  1056.8 118.2 %all-reduce.24.cloned.1.call-start = ((), (), s32[]{:S(2)}) async-start(), calls=%async_computation.3 | async-start | bytes 524288 | tf_op jit(solution)/shard_map/psum | solution.py:117
  1112.6 3.8 copy-start.5
  1119.5 241.6 %all-gather.7.cloned.1.call-start = ((), (), s32[]{:S(2)}) async-start(), calls=%async_computation.5 | async-start | bytes 23592960 | tf_op jit(solution)/shard_map/all_gather | solution.py:120
  1375.1 2.8 copy-start.6
  (5 other events, 8.3 us)
Sparse Core Ops, SparseCore 0:
  124.8 59.0 all-reduce.35
  189.3 56.6 all-reduce.31
  315.8 68.4 all-reduce.29
  413.2 55.6 all-reduce.17
  475.9 55.4 all-reduce.19
  532.8 184.4 all-gather.4
  784.7 54.5 all-reduce.33
  844.7 56.7 all-reduce.27
  971.9 68.4 all-reduce.25
  1056.9 55.6 all-reduce.21
  1119.6 55.3 all-reduce.23
  1176.5 184.4 all-gather.6
